TPU v7x, 128 devices: a whole 4x4x4 slice. The times are simulated.
128 devices in a mesh: gx: 16 (over z, x), gy: 8 (over y, core).
Axes of the slice: x: 4, y: 4, z: 4, core: 2. Of those that a mesh axis runs over, the one named last changes fastest.
Arguments:
- positions: float32 [3, 262144], P(None, ('gx', 'gy')), may hold values from -6 to 6
- velocities: float32 [3, 262144], P(None, ('gx', 'gy')), may hold values from -6 to 6
- masses: float32 [262144], P(('gx', 'gy')), may hold values from 0.25 to 4
- labels: int32 [262144, 1], P(('gx', 'gy')), may hold values from 0 to 1023; in each aligned block of 2048 rows (0 to 2047, 2048 to 4095, ...) at most 4 rows name the same one
- owner_slot: int32 [1024], replicated, may hold values from 0 to 1023, each once
- group_cap: int32 [1024], replicated, may hold values from 512 to 4095
Outputs:
- compact_index: int32 [262144], P(('gx', 'gy'))
- potential: float32 [262144], P(('gx', 'gy'))
- binding: float32 [262144], P(('gx', 'gy'))
- catalog: float32 [4, 1024], P(None, ('gx', 'gy'))
Inputs may be any that keep to these rules, and one draw needn't show every extreme that they name: `labels`: on each device's 2048 particles no label occurs more than 4 times; some label occurs exactly 4 times in some devices' particles; every label occurs somewhere. `owner_slot` is a permutation. Group g is owned by device owner_slot[g] // 8 (devices numbered along gx then gy) as its local group owner_slot[g] % 8.
All inputs are finite; a program needn't handle non-finite values.
Results may differ from a plain program's by a relative error of at most 0.0003.
Values sent between devices are 32-bit elements; how exact they have to be, the bound alone decides.
A program may use at most 64 MiB of HBM per device.

v0:
```python
import jax
import jax.numpy as jnp
from jax import lax
from jax.sharding import PartitionSpec as P

CAP = 2048
softening_sq = 0.0025


def potential_of(group_block, live_count):
    coords = group_block[0:3]
    weights = group_block[6]
    width = min(512, CAP)
    block_count = (live_count + width - 1) // width

    def row_step(row_block, result):
        row_start = row_block * width
        near = lax.dynamic_slice_in_dim(coords, row_start, width, 1)
        row_ids = row_start + jnp.arange(width, dtype=jnp.int32)

        def column_step(column_block, accum):
            column_start = column_block * width
            other = lax.dynamic_slice_in_dim(coords, column_start, width, 1)
            other_mass = lax.dynamic_slice_in_dim(weights, column_start, width, 0)
            column_ids = column_start + jnp.arange(width, dtype=jnp.int32)
            dist_sq = jnp.sum((near[:, :, None] - other[:, None, :]) ** 2, axis=0)
            inverse = jnp.where(
                row_ids[:, None] == column_ids[None, :], 0.0, lax.rsqrt(dist_sq + softening_sq)
            )
            return accum + jnp.sum(inverse * other_mass[None, :], axis=1)

        accum = lax.fori_loop(0, block_count, column_step, jnp.zeros((width,), jnp.float32))
        return lax.dynamic_update_slice_in_dim(result, -accum / CAP, row_start, 0)

    return lax.fori_loop(0, block_count, row_step, jnp.zeros((CAP,), jnp.float32))


def owner_work(received):
    items = received.shape[0]
    member_ranks = received[:, 7, :]
    valid = member_ranks >= 0.0
    target = jnp.where(valid, member_ranks.astype(jnp.int32), CAP)
    compact = (
        jnp.zeros((items, 7, CAP), jnp.float32)
        .at[jnp.arange(items)[:, None, None], jnp.arange(7)[None, :, None], target[:, None, :]]
        .set(received[:, 0:7, :], mode="drop")
    )
    live = jnp.sum(valid, axis=1, dtype=jnp.int32)
    pot = lax.map(lambda packed: potential_of(packed[0], packed[1]), (compact, live))
    weights = compact[:, 6, :]
    mass_sum = jnp.sum(weights, axis=1)
    bulk = jnp.sum(weights[:, None, :] * compact[:, 3:6, :], axis=2) / mass_sum[:, None]
    energy = 0.5 * jnp.sum((compact[:, 3:6, :] - bulk[:, :, None]) ** 2, axis=1) + pot
    both = jnp.stack([pot, energy], axis=1)
    safe = jnp.broadcast_to(jnp.minimum(target, CAP - 1)[:, None, :], (items, 2, target.shape[1]))
    answers = jnp.where(valid[:, None, :], jnp.take_along_axis(both, safe, axis=2), 0.0)
    stats = jnp.concatenate([mass_sum[:, None] / CAP, bulk], axis=1)
    return (answers, stats)


def shards(positions, velocities, masses, labels, owner_slot, group_cap):
    label_flat = labels[:, 0]
    count_dev = label_flat.shape[0]
    ngroups = owner_slot.shape[0]
    devices = lax.axis_size(("gx", "gy"))
    owned = ngroups // devices
    most_rows = 2 * count_dev // ngroups
    width_all = devices * most_rows
    row_width = min(512, count_dev)
    row_blocks = count_dev // row_width
    group_ids = jnp.arange(ngroups, dtype=jnp.int32)
    particle_ids = jnp.arange(count_dev, dtype=jnp.int32)
    block_starts = jnp.arange(row_blocks, dtype=jnp.int32) * row_width

    def tally(row_start):
        rows_label = lax.dynamic_slice_in_dim(label_flat, row_start, row_width, 0)
        rows_ids = row_start + jnp.arange(row_width, dtype=jnp.int32)
        same = (rows_label[:, None] == label_flat[None, :]) & (
            particle_ids[None, :] < rows_ids[:, None]
        )
        earlier = jnp.sum(same, axis=1, dtype=jnp.int32)
        hits = jnp.sum(rows_label[:, None] == group_ids[None, :], axis=0, dtype=jnp.int32)
        return (earlier, hits)

    earlier, hits = lax.map(tally, block_starts)
    local_rank = earlier.reshape(count_dev)
    counts = jnp.sum(hits, axis=0, dtype=jnp.int32)
    table = lax.all_gather(counts[None, :], ("gx", "gy"), axis=0, tiled=True)
    position = lax.axis_index(("gx", "gy"))
    below = (jnp.arange(devices, dtype=jnp.int32) < position)[:, None]
    prefix = jnp.sum(jnp.where(below, table, 0), axis=0, dtype=jnp.int32)
    totals = jnp.sum(table, axis=0, dtype=jnp.int32)
    limits = jnp.minimum(group_cap, CAP)
    kept_counts = jnp.minimum(totals, limits)
    starts = jnp.cumsum(kept_counts) - kept_counts
    lookup = jnp.stack([prefix, limits, starts, owner_slot], axis=1).astype(jnp.float32)

    def fetch(row_start):
        rows_label = lax.dynamic_slice_in_dim(label_flat, row_start, row_width, 0)
        onehot = (rows_label[:, None] == group_ids[None, :]).astype(jnp.float32)
        return jnp.dot(
            onehot, lookup, precision=lax.Precision.HIGHEST, preferred_element_type=jnp.float32
        )

    fetched = lax.map(fetch, block_starts).reshape(count_dev, 4).astype(jnp.int32)
    global_rank = fetched[:, 0] + local_rank
    keep = global_rank < fetched[:, 1]
    compact_index = jnp.where(keep, fetched[:, 2] + global_rank, -1)
    owner = fetched[:, 3] // owned
    local_group = fetched[:, 3] % owned
    dest = jnp.where(keep, owner * most_rows + local_rank, width_all)
    fields = jnp.concatenate(
        [positions, velocities, masses[None, :], global_rank.astype(jnp.float32)[None, :]], axis=0
    )
    outgoing = jnp.zeros((owned, 8, width_all), jnp.float32).at[:, 7, :].set(-1.0)
    outgoing = outgoing.at[local_group[:, None], jnp.arange(8)[None, :], dest[:, None]].set(
        jnp.transpose(fields), mode="drop"
    )
    answers, stats = owner_work(
        lax.all_to_all(outgoing, ("gx", "gy"), split_axis=2, concat_axis=2, tiled=True)
    )
    returned, stats = (
        lax.all_to_all(answers, ("gx", "gy"), split_axis=2, concat_axis=2, tiled=True),
        stats,
    )
    safe_dest = jnp.minimum(dest, width_all - 1)
    values = returned[local_group, :, safe_dest]
    potential = jnp.where(keep, values[:, 0], 0.0)
    binding = jnp.where(keep, values[:, 1], 0.0)
    catalog = jnp.transpose(stats)
    return (compact_index, potential, binding, catalog)


def solution(mesh):
    return jax.shard_map(
        shards,
        mesh=mesh,
        in_specs=(
            P(None, ("gx", "gy")),
            P(None, ("gx", "gy")),
            P(("gx", "gy")),
            P(("gx", "gy"), None),
            P(),
            P(),
        ),
        out_specs=(P(("gx", "gy")), P(("gx", "gy")), P(("gx", "gy")), P(None, ("gx", "gy"))),
        check_vma=False,
    )
```

profile of v0, /device:TPU:1, one launch (start us, length us, event | category | flops | bytes accessed | tf_op | source)
XLA Modules:
  0.0 398.8 jit_solution(8188834028946037595)
XLA Ops:
  0.7 24.2 %while.85 = (s32[]{:T(128)}, s32[4,512]{1,0:T(4,128)S(1)}, s32[4,1024]{1,0:T(4,128)S(1)}, s32[4]{0:T(128)S(1)}, s32[2048]{0:T(1024)}, /*index=5*/s32[2048,1]{0,1:T(1,128)}, s32[]{:T(128)}, s32[]{:T(128)}, s32[]{:T(128)}) while((s32[]{:T(128)}, s32[4,512]{1,0:T(4,128)S(1)}, s32[4,1024]{1,0:T(4,128)S(1)}, s32[4]{0:T(128)S(1)}, ...), condition=%wide.region_3.4_spmd.clone, body=%wide.region_0.3_spmd.clone.sunk | while | flops 6814725 | bytes 39067 | solution.py:85
  3.2 0.8 dynamic_slice.62
  4.7 1.7 convert_reduce_fusion.5
  9.3 0.8 dynamic_slice.62
  10.7 1.7 convert_reduce_fusion.5
  16.8 1.7 convert_reduce_fusion.5
  22.8 1.7 convert_reduce_fusion.5
  24.9 39.5 %all-gather = s32[131072]{0:T(1024)S(1)} all-gather(s32[1024]{0:T(1024)S(1)} %reduce_sum.99), channel_id=2, replica_groups=mesh['gx'=16,'gy'=8] {'gx','gy'}, dimensions={0}, use_global_device_ids=true | all-gather | bytes 528384 | tf_op jit(solution)/shard_map/all_gather | solution.py:88
  65.3 17.6 %while.86 = (s32[]{:T(128)}, f32[4,512,4]{1,2,0:T(4,128)S(1)}, s32[4]{0:T(128)S(1)}, s32[2048]{0:T(1024)}, f32[1024,4]{0,1:T(4,128)S(1)}, /*index=5*/s32[]{:T(128)}, s32[]{:T(128)}, s32[]{:T(128)}) while((s32[]{:T(128)}, f32[4,512,4]{1,2,0:T(4,128)S(1)}, s32[4]{0:T(128)S(1)}, s32[2048]{0:T(1024)}, f32[1024,4]{0,1:T(4,128)S(1)}, ...), condition=%wide.region_10.11_spmd.clone, body=%wide.region_9.10_spmd.clone.sunk | while | flops 25690116 | bytes 30859 | solution.py:105
  67.8 0.8 dynamic_slice.64
  68.6 1.1 fusion.34
  72.2 0.8 dynamic_slice.64
  73.0 1.1 fusion.34
  77.4 1.1 fusion.34
  81.8 1.1 fusion.34
  85.2 60.4 %scatter_fusion = f32[32768]{0:T(1024)S(1)} fusion(f32[32768]{0:T(1024)S(1)} %copy-done, s32[16384]{0:T(1024)S(1)} %reshape.207, f32[16384]{0:T(1024)S(1)} %reshape.209), kind=kCustom, calls=%fused_computation.2 | custom fusion | bytes 262144
  146.4 1.7 reshape.225
  148.1 5.2 %all-to-all-start = ((f32[128,1,256]{2,1,0:T(1,128)}), f32[128,1,256]{2,1,0:T(1,128)S(1)}, u32[]{:S(2)}, u32[]{:S(2)}) async-start(f32[128,1,256]{2,1,0:T(1,128)} %reshape.225), calls=%async_computation | async-start | bytes 262144 | tf_op jit(solution)/shard_map/all_to_all | solution.py:120
  153.4 10.0 %all-to-all-done = f32[128,1,256]{2,1,0:T(1,128)S(1)} async-done(((f32[128,1,256]{2,1,0:T(1,128)}), f32[128,1,256]{2,1,0:T(1,128)S(1)}, u32[]{:S(2)}, u32[]{:S(2)}) %all-to-all-start) | async-done | bytes 131104 | tf_op jit(solution)/shard_map/all_to_all | solution.py:120
  163.8 1.0 reduce.18
  164.8 1.1 reshape.226
  166.0 2.0 slice.104
  167.9 2.2 copy.43
  171.5 105.3 %scatter_custom_fusion.1 = f32[114688]{0:T(1024)S(1)} fusion(s32[28672]{0:T(1024)S(1)} %reshape.213, f32[28672]{0:T(1024)S(1)} %reshape.215, f32[]{:T(128)} %constant.239.clone.1), kind=kCustom, calls=%fused_computation.35 | custom fusion | bytes 458756
  277.3 20.6 %while.84 = (s32[]{:T(128)}, f32[8,2048]{1,0:T(8,128)S(1)}, s32[8]{0:T(128)S(1)}, f32[8,7,2048]{2,0,1:T(8,128)S(1)}, s32[]{:T(128)}, /*index=5*/s32[]{:T(128)}, ...) while((s32[]{:T(128)}, f32[8,2048]{1,0:T(8,128)S(1)}, ...), condition=%wide.region_21.22_spmd, body=%wide.region_14.21_spmd.sunk | while | flops 3409951 | bytes 2302925 | solution.py:49
  278.7 1.0 while.87
  278.7 0.8 while.88
  281.2 1.0 while.87
  281.3 0.8 while.88
  283.8 1.0 while.87
  283.9 0.8 while.88
  286.4 1.0 while.87
  286.4 0.8 while.88
  289.0 1.0 while.87
  289.0 0.8 while.88
  291.5 1.0 while.87
  291.6 0.8 while.88
  294.1 1.0 while.87
  294.1 0.8 while.88
  296.7 1.0 while.87
  296.7 0.8 while.88
  297.9 63.1 %gather_fusion.1 = f32[8192]{0:T(1024)S(1)} fusion(f32[8,2,2048]{2,0,1:T(8,128)S(1)} %pad_maximum_fusion, s32[8192]{0:T(1024)S(1)} %bitcast.99), kind=kCustom, calls=%fused_computation.1 | custom fusion | bytes 163840 | tf_op jit(solution)/shard_map/jit(take_along_axis)/gather | solution.py:56
  361.1 1.0 copy.40
  362.1 4.1 %all-to-all-start.1 = ((f32[8,2,512]{0,1,2:T(2,128)}), f32[8,2,512]{0,1,2:T(2,128)S(1)}, u32[]{:S(2)}, u32[]{:S(2)}) async-start(f32[8,2,512]{0,1,2:T(2,128)} %copy.40), calls=%async_computation.1 | async-start | bytes 1048576 | tf_op jit(solution)/shard_map/all_to_all | solution.py:123
  366.8 13.0 %all-to-all-done.1 = f32[8,2,512]{0,1,2:T(2,128)S(1)} async-done(((f32[8,2,512]{0,1,2:T(2,128)}), f32[8,2,512]{0,1,2:T(2,128)S(1)}, u32[]{:S(2)}, u32[]{:S(2)}) %all-to-all-start.1) | async-done | bytes 32800 | tf_op jit(solution)/shard_map/all_to_all | solution.py:123
  379.8 3.2 copy.41
  383.0 13.0 %gather_fusion = f32[2048,2]{1,0:T(8,128)S(1)} fusion(f32[8,2,512]{1,2,0:T(8,128)S(1)} %copy.41, s32[2048]{0:T(1024)S(1)} %bitcast.100), kind=kCustom, calls=%fused_computation | custom fusion | bytes 49152 | tf_op jit(solution)/shard_map/gather | solution.py:127
  396.1 0.9 slice_reduce_fusion
  (234 shorter events, 34.4 us)
Async XLA Ops:
  0.6 64.0 %copy-start.3 = (s32[1024]{0:T(1024)S(1)}, s32[1024]{0:T(1024)}, u32[]{:S(2)}) copy-start(s32[1024]{0:T(1024)} %param.23) | copy-start | bytes 12292
  0.6 64.6 %copy-start.5 = (s32[1024]{0:T(1024)S(1)}, s32[1024]{0:T(1024)}, u32[]{:S(2)}) copy-start(s32[1024]{0:T(1024)} %param.22) | copy-start | bytes 12292
  64.5 18.7 %copy-start.8 = (s32[3]{0:T(128)S(1)}, s32[3]{0:T(128)}, u32[]{:S(2)}) copy-start(s32[3]{0:T(128)} %constant.257) | copy-start | bytes 40
  64.5 18.7 %copy-start.7 = (s32[3]{0:T(128)S(1)}, s32[3]{0:T(128)}, u32[]{:S(2)}) copy-start(s32[3]{0:T(128)} %constant.260) | copy-start | bytes 40
  82.9 1.4 copy-start.1
  82.9 1.4 copy-start.2
  82.9 1.4 copy-start.4
  83.7 1.4 copy-start
  148.1 15.3 %all-to-all-start = ((f32[128,1,256]{2,1,0:T(1,128)}), f32[128,1,256]{2,1,0:T(1,128)S(1)}, u32[]{:S(2)}, u32[]{:S(2)}) async-start(f32[128,1,256]{2,1,0:T(1,128)} %reshape.225), calls=%async_computation | async-start | bytes 262144 | tf_op jit(solution)/shard_map/all_to_all | solution.py:120
  167.9 2.5 copy-start.9
  167.9 2.6 copy-start.6
  362.1 17.7 %all-to-all-start.1 = ((f32[8,2,512]{0,1,2:T(2,128)}), f32[8,2,512]{0,1,2:T(2,128)S(1)}, u32[]{:S(2)}, u32[]{:S(2)}) async-start(f32[8,2,512]{0,1,2:T(2,128)} %copy.40), calls=%async_computation.1 | async-start | bytes 1048576 | tf_op jit(solution)/shard_map/all_to_all | solution.py:123
where the time goes:
time: 400 us; the launch traced here: 399 us
  local copies, waits for them, and re-layouts  277 us (69%)
  blocking collectives  39.5 us (10%)
  waiting for transfers between devices  22.9 us (6%)
  loops' own time  22.3 us (6%)
  other arithmetic  22.1 us (6%)
  starting transfers between devices  9.36 us (2%)
  matrix products  4.35 us (1%)
    unnamed x33, local copies, waits for them, and re-layouts  172 us
    gather x2, local copies, waits for them, and re-layouts, owner_work(): jnp.take_along_axis(both, safe, axis=2)  63.1 us
    all_gather x1, blocking collectives, shards(): table = lax.all_gather(counts[None, :], ('gx', 'gy'), axis=0, tiled=True)  39.5 us
    gather x1, local copies, waits for them, and re-layouts, shards(): values = returned[local_group, :, safe_dest]  13 us
    all_to_all x1, waiting for transfers between devices, shards(): lax.all_to_all(answers, ('gx', 'gy'), split_axis=2, concat_axis=2, tiled=...  13 us
    all_to_all x1, waiting for transfers between devices, shards(): lax.all_to_all(outgoing, ('gx', 'gy'), split_axis=2, concat_axis=2, tiled...  9.98 us
  transfers between devices with their start and end apart: 2, of which 2 were waited for; matrix products, arithmetic and copies ran while one was open for 0% of the time, Pallas kernels for 0%

commit v1 on v0

--- a/solution.py
+++ b/solution.py
@@ -85,7 +85,12 @@
     earlier, hits = lax.map(tally, block_starts)
     local_rank = earlier.reshape(count_dev)
     counts = jnp.sum(hits, axis=0, dtype=jnp.int32)
-    table = lax.all_gather(counts[None, :], ("gx", "gy"), axis=0, tiled=True)
+    table = jnp.concatenate(
+        lax.all_to_all(
+            jnp.stack([counts[None, :]] * lax.axis_size(("gx", "gy"))), ("gx", "gy"), 0, 0
+        ),
+        axis=0,
+    )
     position = lax.axis_index(("gx", "gy"))
     below = (jnp.arange(devices, dtype=jnp.int32) < position)[:, None]
     prefix = jnp.sum(jnp.where(below, table, 0), axis=0, dtype=jnp.int32)

time: 400 us -> 386 us (0.965)
  blocking collectives: 39.5 us -> 0 us
  waiting for transfers between devices: 22.9 us -> 36.5 us
  starting transfers between devices: 9.36 us -> 20.1 us
    all_gather x1 -> x0, blocking collectives: 39.5 us -> none  [shards(): table = lax.all_gather(counts[None, :], ('gx', 'gy'), axis=0, tiled=True)]
    all_to_all x0 -> x1, waiting for transfers between devices: none -> 13.5 us  [shards(): lax.all_to_all(jnp.stack([counts[None, :]] * lax.axis_size(('gx', 'gy')))...]
    all_to_all x0 -> x1, starting transfers between devices: none -> 11.5 us  [shards(): lax.all_to_all(jnp.stack([counts[None, :]] * lax.axis_size(('gx', 'gy')))...]
  transfers between devices with their start and end apart: 2 -> 3, of which waited for: 2 -> 3; matrix products, arithmetic and copies ran while one was open for 0% -> 0% of each run, Pallas kernels for 0% -> 0%
where the time goes in v1:
time: 386 us; the launch traced here: 385 us
  local copies, waits for them, and re-layouts  278 us (72%)
  waiting for transfers between devices  36.5 us (9%)
  other arithmetic  22.5 us (6%)
  loops' own time  22.3 us (6%)
  starting transfers between devices  20.1 us (5%)
  matrix products  4.35 us (1%)
    unnamed x33, local copies, waits for them, and re-layouts  172 us
    gather x2, local copies, waits for them, and re-layouts, owner_work(): jnp.take_along_axis(both, safe, axis=2)  63.1 us
    all_to_all x1, waiting for transfers between devices, shards(): lax.all_to_all(jnp.stack([counts[None, :]] * lax.axis_size(('gx', 'gy')))...  13.5 us
    gather x1, local copies, waits for them, and re-layouts, shards(): values = returned[local_group, :, safe_dest]  13 us
    all_to_all x1, waiting for transfers between devices, shards(): lax.all_to_all(answers, ('gx', 'gy'), split_axis=2, concat_axis=2, tiled=...  13 us
    all_to_all x1, starting transfers between devices, shards(): lax.all_to_all(jnp.stack([counts[None, :]] * lax.axis_size(('gx', 'gy')))...  11.5 us
    all_to_all x1, waiting for transfers between devices, shards(): lax.all_to_all(outgoing, ('gx', 'gy'), split_axis=2, concat_axis=2, tiled...  10 us
    another operation x1, loops' own time, shards(): earlier, hits = lax.map(tally, block_starts)  7.94 us
  transfers between devices with their start and end apart: 3, of which 3 were waited for; matrix products, arithmetic and copies ran while one was open for 0% of the time, Pallas kernels for 0%

profile of v1, /device:TPU:1, one launch (start us, length us, event | category | flops | bytes accessed | tf_op | source)
XLA Modules:
  0.0 385.0 jit_solution(16024207797259200826)
XLA Ops:
  0.7 24.2 %while.85 = (s32[]{:T(128)}, s32[4,512]{1,0:T(4,128)S(1)}, s32[4,1024]{1,0:T(4,128)S(1)}, s32[4]{0:T(128)S(1)}, s32[2048]{0:T(1024)}, /*index=5*/s32[2048,1]{0,1:T(1,128)}, s32[]{:T(128)}, s32[]{:T(128)}, s32[]{:T(128)}) while((s32[]{:T(128)}, s32[4,512]{1,0:T(4,128)S(1)}, s32[4,1024]{1,0:T(4,128)S(1)}, s32[4]{0:T(128)S(1)}, ...), condition=%wide.region_3.4_spmd.clone, body=%wide.region_0.3_spmd.clone.sunk | while | flops 6814725 | bytes 39067 | solution.py:85
  4.7 1.7 convert_reduce_fusion.5
  10.7 1.7 convert_reduce_fusion.5
  16.7 1.7 convert_reduce_fusion.5
  22.8 1.7 convert_reduce_fusion.5
  24.9 1.1 stack.27
  26.0 11.5 %all-to-all-start = ((s32[128,1,1024]{2,1,0:T(1,128)}), s32[128,1,1024]{2,1,0:T(1,128)S(1)}, u32[]{:S(2)}, u32[]{:S(2)}) async-start(s32[128,1,1024]{2,1,0:T(1,128)} %stack.27), calls=%async_computation | async-start | bytes 1048576 | tf_op jit(solution)/shard_map/all_to_all | solution.py:89
  37.5 13.5 %all-to-all-done = s32[128,1,1024]{2,1,0:T(1,128)S(1)} async-done(((s32[128,1,1024]{2,1,0:T(1,128)}), s32[128,1,1024]{2,1,0:T(1,128)S(1)}, u32[]{:S(2)}, u32[]{:S(2)}) %all-to-all-start) | async-done | bytes 524320 | tf_op jit(solution)/shard_map/all_to_all | solution.py:89
  52.2 17.6 %while.86 = (s32[]{:T(128)}, f32[4,512,4]{1,2,0:T(4,128)S(1)}, s32[4]{0:T(128)S(1)}, s32[2048]{0:T(1024)}, f32[1024,4]{0,1:T(4,128)S(1)}, /*index=5*/s32[]{:T(128)}, s32[]{:T(128)}, s32[]{:T(128)}) while((s32[]{:T(128)}, f32[4,512,4]{1,2,0:T(4,128)S(1)}, s32[4]{0:T(128)S(1)}, s32[2048]{0:T(1024)}, f32[1024,4]{0,1:T(4,128)S(1)}, ...), condition=%wide.region_10.11_spmd.clone, body=%wide.region_9.10_spmd.clone.sunk | while | flops 25690116 | bytes 30859 | solution.py:110
  54.7 0.8 dynamic_slice.64
  55.5 1.1 fusion.35
  59.1 0.8 dynamic_slice.64
  59.9 1.1 fusion.35
  64.3 1.1 fusion.35
  68.7 1.1 fusion.35
  72.1 60.4 %scatter_fusion = f32[32768]{0:T(1024)S(1)} fusion(f32[32768]{0:T(1024)S(1)} %copy-done, s32[16384]{0:T(1024)S(1)} %reshape.213, f32[16384]{0:T(1024)S(1)} %reshape.215), kind=kCustom, calls=%fused_computation.2 | custom fusion | bytes 262144
  133.3 1.7 reshape.230
  135.0 4.5 %all-to-all-start.1 = ((f32[128,1,256]{2,1,0:T(1,128)}), f32[128,1,256]{2,1,0:T(1,128)S(1)}, u32[]{:S(2)}, u32[]{:S(2)}) async-start(f32[128,1,256]{2,1,0:T(1,128)} %reshape.230), calls=%async_computation.1 | async-start | bytes 262144 | tf_op jit(solution)/shard_map/all_to_all | solution.py:125
  139.5 10.0 %all-to-all-done.1 = f32[128,1,256]{2,1,0:T(1,128)S(1)} async-done(((f32[128,1,256]{2,1,0:T(1,128)}), f32[128,1,256]{2,1,0:T(1,128)S(1)}, u32[]{:S(2)}, u32[]{:S(2)}) %all-to-all-start.1) | async-done | bytes 131104 | tf_op jit(solution)/shard_map/all_to_all | solution.py:125
  150.1 1.0 reduce.19
  151.0 1.1 reshape.231
  152.2 2.0 slice.104
  154.1 2.2 copy.44
  157.7 105.3 %scatter_custom_fusion.1 = f32[114688]{0:T(1024)S(1)} fusion(s32[28672]{0:T(1024)S(1)} %reshape.219, f32[28672]{0:T(1024)S(1)} %reshape.221, f32[]{:T(128)} %constant.239.clone.1), kind=kCustom, calls=%fused_computation.36 | custom fusion | bytes 458756
  263.5 20.6 %while.84 = (s32[]{:T(128)}, f32[8,2048]{1,0:T(8,128)S(1)}, s32[8]{0:T(128)S(1)}, f32[8,7,2048]{2,0,1:T(8,128)S(1)}, s32[]{:T(128)}, /*index=5*/s32[]{:T(128)}, ...) while((s32[]{:T(128)}, f32[8,2048]{1,0:T(8,128)S(1)}, ...), condition=%wide.region_21.22_spmd, body=%wide.region_14.21_spmd.sunk | while | flops 3409951 | bytes 2302925 | solution.py:49
  264.9 1.0 while.87
  264.9 0.8 while.88
  267.5 1.0 while.87
  267.5 0.8 while.88
  270.0 1.0 while.87
  270.1 0.8 while.88
  272.6 1.0 while.87
  272.6 0.8 while.88
  275.2 1.0 while.87
  275.2 0.8 while.88
  277.7 1.0 while.87
  277.8 0.8 while.88
  280.3 1.0 while.87
  280.4 0.8 while.88
  282.9 1.0 while.87
  282.9 0.8 while.88
  284.1 63.1 %gather_fusion.1 = f32[8192]{0:T(1024)S(1)} fusion(f32[8,2,2048]{2,0,1:T(8,128)S(1)} %pad_maximum_fusion, s32[8192]{0:T(1024)S(1)} %bitcast.103), kind=kCustom, calls=%fused_computation.1 | custom fusion | bytes 163840 | tf_op jit(solution)/shard_map/jit(take_along_axis)/gather | solution.py:56
  347.3 1.0 copy.40
  348.3 4.1 %all-to-all-start.2 = ((f32[8,2,512]{0,1,2:T(2,128)}), f32[8,2,512]{0,1,2:T(2,128)S(1)}, u32[]{:S(2)}, u32[]{:S(2)}) async-start(f32[8,2,512]{0,1,2:T(2,128)} %copy.40), calls=%async_computation.2 | async-start | bytes 1048576 | tf_op jit(solution)/shard_map/all_to_all | solution.py:128
  353.0 13.0 %all-to-all-done.2 = f32[8,2,512]{0,1,2:T(2,128)S(1)} async-done(((f32[8,2,512]{0,1,2:T(2,128)}), f32[8,2,512]{0,1,2:T(2,128)S(1)}, u32[]{:S(2)}, u32[]{:S(2)}) %all-to-all-start.2) | async-done | bytes 32800 | tf_op jit(solution)/shard_map/all_to_all | solution.py:128
  366.0 3.2 copy.41
  369.2 13.0 %gather_fusion = f32[2048,2]{1,0:T(8,128)S(1)} fusion(f32[8,2,512]{1,2,0:T(8,128)S(1)} %copy.41, s32[2048]{0:T(1024)S(1)} %bitcast.104), kind=kCustom, calls=%fused_computation | custom fusion | bytes 49152 | tf_op jit(solution)/shard_map/gather | solution.py:132
  382.3 0.9 slice_reduce_fusion
  (236 shorter events, 36.3 us)
Async XLA Ops:
  0.6 50.7 %copy-start.3 = (s32[1024]{0:T(1024)S(1)}, s32[1024]{0:T(1024)}, u32[]{:S(2)}) copy-start(s32[1024]{0:T(1024)} %param.23) | copy-start | bytes 12292
  0.6 51.5 %copy-start.5 = (s32[1024]{0:T(1024)S(1)}, s32[1024]{0:T(1024)}, u32[]{:S(2)}) copy-start(s32[1024]{0:T(1024)} %param.22) | copy-start | bytes 12292
  26.0 25.0 %all-to-all-start = ((s32[128,1,1024]{2,1,0:T(1,128)}), s32[128,1,1024]{2,1,0:T(1,128)S(1)}, u32[]{:S(2)}, u32[]{:S(2)}) async-start(s32[128,1,1024]{2,1,0:T(1,128)} %stack.27), calls=%async_computation | async-start | bytes 1048576 | tf_op jit(solution)/shard_map/all_to_all | solution.py:89
  51.4 18.7 %copy-start.8 = (s32[3]{0:T(128)S(1)}, s32[3]{0:T(128)}, u32[]{:S(2)}) copy-start(s32[3]{0:T(128)} %constant.257) | copy-start | bytes 40
  51.9 18.3 %copy-start.7 = (s32[3]{0:T(128)S(1)}, s32[3]{0:T(128)}, u32[]{:S(2)}) copy-start(s32[3]{0:T(128)} %constant.260) | copy-start | bytes 40
  69.8 1.3 copy-start.1
  69.8 1.4 copy-start.2
  69.8 1.4 copy-start.4
  70.3 1.8 copy-start
  135.0 14.6 %all-to-all-start.1 = ((f32[128,1,256]{2,1,0:T(1,128)}), f32[128,1,256]{2,1,0:T(1,128)S(1)}, u32[]{:S(2)}, u32[]{:S(2)}) async-start(f32[128,1,256]{2,1,0:T(1,128)} %reshape.230), calls=%async_computation.1 | async-start | bytes 262144 | tf_op jit(solution)/shard_map/all_to_all | solution.py:125
  154.1 2.5 copy-start.9
  154.1 2.6 copy-start.6
  348.3 17.7 %all-to-all-start.2 = ((f32[8,2,512]{0,1,2:T(2,128)}), f32[8,2,512]{0,1,2:T(2,128)S(1)}, u32[]{:S(2)}, u32[]{:S(2)}) async-start(f32[8,2,512]{0,1,2:T(2,128)} %copy.40), calls=%async_computation.2 | async-start | bytes 1048576 | tf_op jit(solution)/shard_map/all_to_all | solution.py:128
